TPU v7x, 32 devices: a whole 2x2x4 slice. The times are simulated.
32 devices in a mesh: dp: 8 (over z, y), ctx: 4 (over x, core).
Axes of the slice: x: 2, y: 2, z: 4, core: 2. Of those that a mesh axis runs over, the one named last changes fastest.
Arguments:
- projected: bfloat16 [8, 512, 3, 4096], P('dp', 'ctx'), may hold values from -6 to 6
- short_taps: float32 [3, 3, 4096], P(None, None, 'ctx'), may hold values from -3 to 3
- long_filter: bfloat16 [512, 4096], P('dp', 'ctx'), may hold values from -1.1 to 1.1
- skip_gain: float32 [4096], P('ctx'), may hold values from -4 to 4
Outputs:
- mixed: bfloat16 [8, 512, 4096], P('dp', 'ctx')
All inputs are finite; a program needn't handle non-finite values.
Results may differ from a plain program's by a relative error of at most 0.012.
Values may be sent and summed in bfloat16 or wider, within the bound.
A program may use at most 64 MiB of HBM per device.

v0:
```python
import math
import jax
import jax.numpy as jnp
import numpy as np
from jax import lax
from jax.sharding import PartitionSpec as P

RADIX = 64
HIGH = lax.Precision.HIGHEST


def causal_short(extended, taps, kernel_size):
    row_count = extended.shape[0] - (kernel_size - 1)
    widened = extended.astype(jnp.float32)
    summed = jnp.zeros((row_count,) + widened.shape[1:], jnp.float32)
    for tap_index in range(kernel_size):
        offset = kernel_size - 1 - tap_index
        summed = summed + taps[tap_index] * widened[offset : offset + row_count]
    return (summed[:, 0].astype(jnp.bfloat16), (summed[:, 1] * summed[:, 2]).astype(jnp.bfloat16))


def dft_tables(length, radix_size):
    outer_size = 2 * length // radix_size
    total_size = outer_size * radix_size
    outer_range = jnp.arange(outer_size, dtype=jnp.int32)
    inner_range = jnp.arange(radix_size, dtype=jnp.int32)
    angle_one = (
        2.0
        * math.pi
        / outer_size
        * (outer_range[:, None] * outer_range[None, :] % outer_size).astype(jnp.float32)
    )
    angle_twist = (
        2.0
        * math.pi
        / total_size
        * (outer_range[:, None] * inner_range[None, :] % total_size).astype(jnp.float32)
    )
    angle_two = (
        2.0
        * math.pi
        / radix_size
        * (inner_range[:, None] * inner_range[None, :] % radix_size).astype(jnp.float32)
    )
    twist_cos = jnp.cos(angle_twist)[:, :, None]
    twist_sin = jnp.sin(angle_twist)[:, :, None]
    return (
        jnp.cos(angle_one),
        jnp.sin(angle_one),
        twist_cos,
        twist_sin,
        jnp.cos(angle_two),
        jnp.sin(angle_two),
    )


def forward_dft(signal, tables, radix_size):
    cos_one, sin_one, twist_cos, twist_sin, cos_two, sin_two = tables
    outer_size = cos_one.shape[0]
    half_size = outer_size // 2
    block_width = signal.shape[1]
    shaped = signal.reshape(half_size, radix_size * block_width)
    first_re = jnp.dot(cos_one[:, :half_size], shaped, precision=HIGH).reshape(
        outer_size, radix_size, block_width
    )
    first_im = -jnp.dot(sin_one[:, :half_size], shaped, precision=HIGH).reshape(
        outer_size, radix_size, block_width
    )
    second_re = first_re * twist_cos + first_im * twist_sin
    second_im = first_im * twist_cos - first_re * twist_sin
    spec_re = jnp.einsum("amc,mb->abc", second_re, cos_two, precision=HIGH) + jnp.einsum(
        "amc,mb->abc", second_im, sin_two, precision=HIGH
    )
    spec_im = jnp.einsum("amc,mb->abc", second_im, cos_two, precision=HIGH) - jnp.einsum(
        "amc,mb->abc", second_re, sin_two, precision=HIGH
    )
    return (spec_re, spec_im)


def inverse_dft(spec_re, spec_im, tables, radix_size):
    cos_one, sin_one, twist_cos, twist_sin, cos_two, sin_two = tables
    outer_size = cos_one.shape[0]
    half_size = outer_size // 2
    block_width = spec_re.shape[2]
    back_re = jnp.einsum("abc,mb->amc", spec_re, cos_two, precision=HIGH) - jnp.einsum(
        "abc,mb->amc", spec_im, sin_two, precision=HIGH
    )
    back_im = jnp.einsum("abc,mb->amc", spec_re, sin_two, precision=HIGH) + jnp.einsum(
        "abc,mb->amc", spec_im, cos_two, precision=HIGH
    )
    turned_re = (back_re * twist_cos - back_im * twist_sin).reshape(
        outer_size, radix_size * block_width
    )
    turned_im = (back_re * twist_sin + back_im * twist_cos).reshape(
        outer_size, radix_size * block_width
    )
    result = jnp.dot(cos_one[:half_size], turned_re, precision=HIGH) - jnp.dot(
        sin_one[:half_size], turned_im, precision=HIGH
    )
    return result.reshape(half_size * radix_size, block_width) / (outer_size * radix_size)


def long_convolve_blocked(gated_slab, filter_slab):
    length, channels = gated_slab.shape
    block_width = min(128, channels)
    tables = dft_tables(length, RADIX)

    def one_block(block_index, output):
        offset = block_index * block_width
        signal = lax.dynamic_slice_in_dim(gated_slab, offset, block_width, 1).astype(jnp.float32)
        kernel_block = lax.dynamic_slice_in_dim(filter_slab, offset, block_width, 1).astype(
            jnp.float32
        )
        sig_re, sig_im = forward_dft(signal, tables, RADIX)
        ker_re, ker_im = forward_dft(kernel_block, tables, RADIX)
        prod_re = sig_re * ker_re - sig_im * ker_im
        prod_im = sig_re * ker_im + sig_im * ker_re
        result = inverse_dft(prod_re, prod_im, tables, RADIX)
        return lax.dynamic_update_slice_in_dim(output, result, offset, 1)

    return lax.fori_loop(
        0, channels // block_width, one_block, jnp.zeros((length, channels), jnp.float32)
    )


def long_convolve(gated_slab, filter_slab):
    length = gated_slab.shape[0]
    if length > 1024:
        return long_convolve_blocked(gated_slab, filter_slab)
    forward, backward = quarter_tables(length)
    sig = jnp.dot(forward, gated_slab, preferred_element_type=jnp.float32)
    ker = jnp.dot(forward, filter_slab, preferred_element_type=jnp.float32)
    sig_cos, sig_sin, ker_cos, ker_sin = (sig[:length], sig[length:], ker[:length], ker[length:])
    prod = jnp.concatenate(
        [sig_cos * ker_cos - sig_sin * ker_sin, sig_cos * ker_sin + sig_sin * ker_cos]
    ).astype(jnp.bfloat16)
    return jnp.dot(backward, prod, preferred_element_type=jnp.float32)


def quarter_tables(length):
    steps = (4 * np.arange(length)[:, None] + 1) * np.arange(length)[None, :] % (4 * length)
    angles = steps * (2.0 * math.pi / (4 * length))
    table = np.concatenate([np.cos(angles), np.sin(angles)])
    return (jnp.asarray(table, jnp.bfloat16), jnp.asarray(table.T / length, jnp.bfloat16))


def make_response(gated_slab, filter_slab, skip_gain):
    long_part = long_convolve(gated_slab, filter_slab)
    return (long_part + skip_gain * gated_slab.astype(jnp.float32)).astype(jnp.bfloat16)


def combine_rows(query_part, response_part):
    return (query_part.astype(jnp.float32) * response_part.astype(jnp.float32)).astype(jnp.bfloat16)


def on_device(projected, short_taps, long_filter, skip_gain):
    kernel_size = short_taps.shape[0]
    ctx_size = lax.axis_size("ctx")
    rows = projected[0]
    filter_slab = lax.all_gather(long_filter, "dp", axis=0, tiled=True)
    all_taps = lax.all_gather(short_taps, "ctx", axis=2, tiled=True)
    halo = lax.ppermute(
        rows[-(kernel_size - 1) :], "ctx", [(i, i + 1) for i in range(ctx_size - 1)]
    )
    queries, gated = causal_short(jnp.concatenate([halo, rows]), all_taps, kernel_size)
    gated_slab = lax.all_to_all(gated, "ctx", split_axis=1, concat_axis=0, tiled=True)
    response_slab = make_response(gated_slab, filter_slab, skip_gain)
    response = lax.all_to_all(response_slab, "ctx", split_axis=0, concat_axis=1, tiled=True)
    return combine_rows(queries, response)[None]


def solution(mesh):
    return jax.shard_map(
        on_device,
        mesh=mesh,
        in_specs=(P("dp", "ctx", None, None), P(None, None, "ctx"), P("dp", "ctx"), P("ctx")),
        out_specs=P("dp", "ctx", None),
        check_vma=False,
    )
```

profile of v0, /device:TPU:0, one launch (start us, length us, event | category | flops | bytes accessed | tf_op | source)
XLA Modules:
  0.0 98.3 jit_solution(9374394444664084530)
XLA Ops:
  6.5 1.0 slice_bitcast_fusion.3
  7.5 2.4 %collective-permute-start = (bf16[2,3,4096]{2,0,1:T(2,128)(2,1)S(1)}, bf16[2,3,4096]{2,0,1:T(2,128)(2,1)S(1)}, u32[]{:S(2)}, u32[]{:S(2)}) collective-permute-start(bf16[2,3,4096]{2,0,1:T(2,128)(2,1)S(1)} %slice_bitcast_fusion.3), channel_id=1, source_target_pairs={{0,1},{1,2},{2,3},{4,5},{5,6},{6,7},{8,9},{9,10},{10,11},{12,13},{... | collective-permute-start | bytes 147464 | tf_op jit(solution)/shard_map/ppermute | solution.py:162
  9.9 7.1 %all_gather.6 = f32[3,3,4096]{2,1,0:T(4,128)S(1)} all-gather(f32[3,3,1024]{2,1,0:T(4,128)} %param.7), channel_id=1, replica_groups=mesh['dp'=8,'ctx'=4] {'ctx'}, dimensions={2}, use_global_device_ids=true | all-gather | bytes 184320 | tf_op jit(solution)/shard_map/all_gather | solution.py:161
  17.1 3.5 %copy.19 = bf16[1,128,3,4096]{1,3,2,0:T(8,128)(2,1)S(1)} copy(bf16[1,128,3,4096]{3,1,2,0:T(8,128)(2,1)} %param.6) | data formatting | bytes 6291456 | tf_op args[0]
  20.6 2.8 %copy.20 = bf16[2,3,4096]{0,2,1:T(8,128)(2,1)} copy(bf16[2,3,4096]{2,0,1:T(2,128)(2,1)S(1)} %collective-permute-done) | data formatting | bytes 98304 | tf_op jit(solution)/shard_map/ppermute | solution.py:162
  23.4 4.1 %maximum_convert_fusion = f32[130,3,4096]{0,2,1:T(8,128)S(1)} fusion(bf16[128,3,4096]{0,2,1:T(8,128)(2,1)S(1)} %bitcast.36, bf16[2,3,4096]{0,2,1:T(8,128)(2,1)} %copy.20), kind=kLoop, calls=%fused_computation.5 | loop fusion | flops 6389760 | bytes 9584640 | tf_op jit(solution)/shard_map/convert_element_type | solution.py:14
  27.5 9.4 %fusion = f32[128,3,4096]{0,2,1:T(8,128)S(1)} fusion(f32[130,3,4096]{0,2,1:T(8,128)S(1)} %maximum_convert_fusion, f32[3,4096]{1,0:T(4,128)S(1)} %get-tuple-element.6, f32[3,4096]{1,0:T(4,128)S(1)} %get-tuple-element.7, f32[3,4096]{1,0:T(4,128)S(1)} %get-tuple-element.5), kind=kLoop, calls=%fused_computation.1 | loop fusion | flops 7864320 | bytes 25313280 | tf_op jit(solution)/shard_map/add | solution.py:18
  36.9 2.7 %copy-done = f32[128,3,4096]{0,2,1:T(8,128)} copy-done((f32[128,3,4096]{0,2,1:T(8,128)}, f32[128,3,4096]{0,2,1:T(8,128)S(1)}, u32[]{:S(2)}) %copy-start) | copy-done | bytes 6291480
  39.5 0.2 fusion.2
  39.7 0.5 copy.21
  40.3 16.9 %all_to_all.29 = bf16[128,4,1024]{2,0,1:T(8,128)(2,1)S(1)} all-to-all(bf16[128,4,1024]{2,0,1:T(8,128)(2,1)S(1)} %copy.21), channel_id=1, replica_groups=mesh['dp'=8,'ctx'=4] {'ctx'}, dimensions={1} | all-to-all | bytes 2097152 | tf_op jit(solution)/shard_map/all_to_all | solution.py:166
  57.2 0.8 copy.22
  58.0 0.3 reshape.46
  58.3 4.5 %fusion.8 = f32[1024,1024]{1,0:T(8,128)} fusion(bf16[1024,512]{1,0:T(8,128)(2,1)} %constant.9, bf16[512,1024]{1,0:T(8,128)(2,1)S(1)} %reshape.46), kind=kOutput, calls=%fused_computation.23 | convolution fusion | flops 1073741824 | bytes 6291456 | tf_op jit(solution)/shard_map/dot_general | solution.py:131
  62.8 2.9 %fusion.9 = f32[1024,1024]{1,0:T(8,128)S(1)} fusion(bf16[1024,512]{1,0:T(8,128)(2,1)} %constant.4.clone, bf16[512,1024]{1,0:T(8,128)(2,1)} %all-gather.2.cloned.1.call-done), kind=kOutput, calls=%fused_computation.24 | convolution fusion | flops 1073741824 | bytes 6291456 | tf_op jit(solution)/shard_map/dot_general | solution.py:132
  65.7 0.0 copy-done.1
  65.8 0.8 fusion.6
  66.6 0.2 copy-done.2
  66.8 0.9 fusion.4
  67.7 16.9 %all_to_all.30 = bf16[4,128,1024]{2,1,0:T(8,128)(2,1)S(1)} all-to-all(bf16[4,128,1024]{2,1,0:T(8,128)(2,1)S(1)} %bitcast.38), channel_id=1, replica_groups=mesh['dp'=8,'ctx'=4] {'ctx'}, dimensions={0} | all-to-all | bytes 2097152 | tf_op jit(solution)/shard_map/all_to_all | solution.py:168
  84.6 1.6 %convert_bitcast_fusion = f32[128,4,1024]{2,0,1:T(8,128)} fusion(bf16[4,128,1024]{2,1,0:T(8,128)(2,1)S(1)} %all_to_all.30), kind=kLoop, calls=%fused_computation.14 | loop fusion | flops 524288 | bytes 3145728 | tf_op jit(solution)/shard_map/convert_element_type | solution.py:153
  86.1 1.9 %copy.23 = f32[128,4,1024]{0,2,1:T(8,128)S(1)} copy(f32[128,4,1024]{2,0,1:T(8,128)} %convert_bitcast_fusion) | data formatting | bytes 4194304 | tf_op jit(solution)/shard_map/convert_element_type | solution.py:153
  88.1 2.0 %fusion.5 = bf16[1,128,4096]{1,2,0:T(8,128)(2,1)S(1)} fusion(f32[128,4,1024]{0,2,1:T(8,128)S(1)} %copy.23, f32[128,3,4096]{0,2,1:T(8,128)} %copy-done), kind=kLoop, calls=%fused_computation.13 | loop fusion | flops 1572864 | bytes 4194304 | tf_op jit(solution)/shard_map/convert_element_type | solution.py:153
  90.1 1.3 %copy.24 = bf16[1,128,4096]{2,1,0:T(8,128)(2,1)} copy(bf16[1,128,4096]{1,2,0:T(8,128)(2,1)S(1)} %fusion.5) | data formatting | bytes 2097152 | tf_op jit(solution)/shard_map/convert_element_type | solution.py:153
  (12 shorter events, 0.1 us)
Async XLA Ops:
  6.5 56.2 %all-gather.2.cloned.1.call-start = ((), (), s32[]{:S(2)}) async-start(), calls=%async_computation.2 | async-start | bytes 1179648 | tf_op jit(solution)/shard_map/all_gather | solution.py:160
  7.5 13.0 %collective-permute-start = (bf16[2,3,4096]{2,0,1:T(2,128)(2,1)S(1)}, bf16[2,3,4096]{2,0,1:T(2,128)(2,1)S(1)}, u32[]{:S(2)}, u32[]{:S(2)}) collective-permute-start(bf16[2,3,4096]{2,0,1:T(2,128)(2,1)S(1)} %slice_bitcast_fusion.3), channel_id=1, source_target_pairs={{0,1},{1,2},{2,3},{4,5},{5,6},{6,7},{8,9},{9,10},{10,11},{12,13},{... | collective-permute-start | bytes 147464 | tf_op jit(solution)/shard_map/ppermute | solution.py:162
  36.9 2.7 %copy-start = (f32[128,3,4096]{0,2,1:T(8,128)}, f32[128,3,4096]{0,2,1:T(8,128)S(1)}, u32[]{:S(2)}) copy-start(f32[128,3,4096]{0,2,1:T(8,128)S(1)} %fusion) | copy-start | bytes 18874372
  62.8 3.0 %copy-start.3 = (bf16[512,512]{1,0:T(8,128)(2,1)S(1)}, bf16[512,512]{1,0:T(8,128)(2,1)}, u32[]{:S(2)}) copy-start(bf16[512,512]{1,0:T(8,128)(2,1)} %constant.10) | copy-start | bytes 1572868
  62.8 3.0 %copy-start.1 = (f32[1024,1024]{1,0:T(8,128)S(1)}, f32[1024,1024]{1,0:T(8,128)}, u32[]{:S(2)}) copy-start(f32[1024,1024]{1,0:T(8,128)} %fusion.8) | copy-start | bytes 12582916
  65.8 1.0 %copy-start.2 = (bf16[512,512]{1,0:T(8,128)(2,1)S(1)}, bf16[512,512]{1,0:T(8,128)(2,1)}, u32[]{:S(2)}) copy-start(bf16[512,512]{1,0:T(8,128)(2,1)} %constant.11) | copy-start | bytes 1572868
  65.8 1.0 %copy-start.4 = (f32[1024]{0:T(1024)S(1)}, f32[1024]{0:T(1024)}, u32[]{:S(2)}) copy-start(f32[1024]{0:T(1024)} %param.9) | copy-start | bytes 12292
Sparse Core Ops, SparseCore 0:
  10.0 42.7 all-gather.1
where the time goes:
time: 98.7 us; the launch traced here: 98.3 us
  blocking collectives  40.9 us (41%)
  other arithmetic  17.3 us (18%)
  local copies, waits for them, and re-layouts  15.1 us (15%)
  between operations  13.5 us (14%)
  matrix products  9.08 us (9%)
  starting transfers between devices  2.36 us (2%)
    all_to_all x1, blocking collectives, on_device(): lax.all_to_all(gated, 'ctx', split_axis=1, concat_axis=0, tiled=True)  16.9 us
    all_to_all x1, blocking collectives, on_device(): lax.all_to_all(response_slab, 'ctx', split_axis=0, concat_axis=1, tiled=T...  16.9 us
    add x1, other arithmetic, causal_short(): summed = summed + taps[tap_index] * widened[offset:offset + row_count]  9.39 us
    all_gather x1, blocking collectives, on_device(): all_taps = lax.all_gather(short_taps, 'ctx', axis=2, tiled=True)  7.11 us
    unnamed x11, local copies, waits for them, and re-layouts  6.44 us
    dot_general x1, matrix products, long_convolve(): sig = jnp.dot(forward, gated_slab, preferred_element_type=jnp.float32)  4.5 us
    convert_element_type x1, other arithmetic, causal_short(): widened = extended.astype(jnp.float32)  4.08 us
    dot_general x1, matrix products, long_convolve(): ker = jnp.dot(forward, filter_slab, preferred_element_type=jnp.float32)  2.94 us
  transfers between devices with their start and end apart: 2, of which 0 were waited for; matrix products, arithmetic and copies ran while one was open for 27% of the time, Pallas kernels for 0%

commit v1 on v0

--- a/solution.py
+++ b/solution.py
@@ -7,6 +7,16 @@
 
 RADIX = 64
 HIGH = lax.Precision.HIGHEST
+
+
+def gather_by_hops(value, axis, dim):
+    size = lax.axis_size(axis)
+    moving, shards = (value, [value])
+    for _ in range(size - 1):
+        moving = lax.ppermute(moving, axis, [(i, (i + 1) % size) for i in range(size)])
+        shards.insert(0, moving)
+    line = jnp.concatenate(shards, axis=dim)
+    return jnp.roll(line, (lax.axis_index(axis) + 1) * value.shape[dim], axis=dim)
 
 
 def causal_short(extended, taps, kernel_size):
@@ -158,7 +168,7 @@
     ctx_size = lax.axis_size("ctx")
     rows = projected[0]
     filter_slab = lax.all_gather(long_filter, "dp", axis=0, tiled=True)
-    all_taps = lax.all_gather(short_taps, "ctx", axis=2, tiled=True)
+    all_taps = gather_by_hops(short_taps, "ctx", 2)
     halo = lax.ppermute(
         rows[-(kernel_size - 1) :], "ctx", [(i, i + 1) for i in range(ctx_size - 1)]
     )

time: 98.7 us -> 95.2 us (0.965)
  blocking collectives: 40.9 us -> 33.8 us
  starting transfers between devices: 2.36 us -> 5.78 us
    all_gather x1 -> x0, blocking collectives: 7.11 us -> none  [on_device(): all_taps = lax.all_gather(short_taps, 'ctx', axis=2, tiled=True)]
    ppermute x1, starting transfers between devices: 2.36 us -> 4.51 us  [on_device(): lax.ppermute(rows[-(kernel_size - 1):], 'ctx', [(i, i + 1) for i in range...]
    ppermute x0 -> x3, starting transfers between devices: none -> 1.27 us  [gather_by_hops(): lax.ppermute(moving, axis, [(i, (i + 1) % size) for i in range(size)])]
    unnamed x11 -> x20, local copies, waits for them, and re-layouts: 6.44 us -> 6.52 us
  transfers between devices with their start and end apart: 2 -> 5, of which waited for: 0 -> 0; matrix products, arithmetic and copies ran while one was open for 27% -> 29% of each run, Pallas kernels for 0% -> 0%
where the time goes in v1:
time: 95.2 us; the launch traced here: 94.8 us
  blocking collectives  33.8 us (36%)
  other arithmetic  17.3 us (18%)
  local copies, waits for them, and re-layouts  15.2 us (16%)
  between operations  13.6 us (14%)
  matrix products  9.08 us (10%)
  starting transfers between devices  5.78 us (6%)
    all_to_all x1, blocking collectives, on_device(): lax.all_to_all(gated, 'ctx', split_axis=1, concat_axis=0, tiled=True)  16.9 us
    all_to_all x1, blocking collectives, on_device(): lax.all_to_all(response_slab, 'ctx', split_axis=0, concat_axis=1, tiled=T...  16.9 us
    add x1, other arithmetic, causal_short(): summed = summed + taps[tap_index] * widened[offset:offset + row_count]  9.39 us
    unnamed x20, local copies, waits for them, and re-layouts  6.52 us
    ppermute x1, starting transfers between devices, on_device(): lax.ppermute(rows[-(kernel_size - 1):], 'ctx', [(i, i + 1) for i in range...  4.51 us
    dot_general x1, matrix products, long_convolve(): sig = jnp.dot(forward, gated_slab, preferred_element_type=jnp.float32)  4.5 us
    convert_element_type x1, other arithmetic, causal_short(): widened = extended.astype(jnp.float32)  4.11 us
    dot_general x1, matrix products, long_convolve(): ker = jnp.dot(forward, filter_slab, preferred_element_type=jnp.float32)  2.94 us
  transfers between devices with their start and end apart: 5, of which 0 were waited for; matrix products, arithmetic and copies ran while one was open for 29% of the time, Pallas kernels for 0%

profile of v1, /device:TPU:0, one launch (start us, length us, event | category | flops | bytes accessed | tf_op | source)
XLA Modules:
  0.0 94.8 jit_solution(11134149246168826643)
XLA Ops:
  6.5 0.5 collective-permute-start
  7.0 1.0 %slice_bitcast_fusion = bf16[2,3,4096]{2,0,1:T(2,128)(2,1)S(1)} fusion(bf16[1,128,3,4096]{3,1,2,0:T(8,128)(2,1)} %param.6), kind=kLoop, calls=%fused_computation.22 | loop fusion | bytes 98304 | tf_op jit(solution)/shard_map/slice | solution.py:173
  8.0 4.5 %collective-permute-start.3 = (bf16[2,3,4096]{2,0,1:T(2,128)(2,1)S(1)}, bf16[2,3,4096]{2,0,1:T(2,128)(2,1)S(1)}, u32[]{:S(2)}, u32[]{:S(2)}) collective-permute-start(bf16[2,3,4096]{2,0,1:T(2,128)(2,1)S(1)} %slice_bitcast_fusion), channel_id=1, source_target_pairs={{0,1},{1,2},{2,3},{4,5},{5,6},{6,7},{8,9},{9,10},{10,11},{12,13},{... | collective-permute-start | bytes 147464 | tf_op jit(solution)/shard_map/ppermute | solution.py:172
  12.6 3.5 %copy.19 = bf16[1,128,3,4096]{1,3,2,0:T(8,128)(2,1)S(1)} copy(bf16[1,128,3,4096]{3,1,2,0:T(8,128)(2,1)} %param.6) | data formatting | bytes 6291456 | tf_op args[0]
  16.1 2.8 %copy.20 = bf16[2,3,4096]{0,2,1:T(8,128)(2,1)} copy(bf16[2,3,4096]{2,0,1:T(2,128)(2,1)S(1)} %collective-permute-done.3) | data formatting | bytes 98304 | tf_op jit(solution)/shard_map/ppermute | solution.py:172
  18.9 0.8 collective-permute-start.2
  19.7 4.1 %maximum_convert_fusion = f32[130,3,4096]{0,2,1:T(8,128)S(1)} fusion(bf16[128,3,4096]{0,2,1:T(8,128)(2,1)S(1)} %bitcast.36, bf16[2,3,4096]{0,2,1:T(8,128)(2,1)} %copy.20), kind=kLoop, calls=%fused_computation.5 | loop fusion | flops 6389760 | bytes 9584640 | tf_op jit(solution)/shard_map/convert_element_type | solution.py:24
  24.0 9.4 %fusion = f32[128,3,4096]{0,2,1:T(8,128)S(1)} fusion(f32[130,3,4096]{0,2,1:T(8,128)S(1)} %maximum_convert_fusion, f32[3,4096]{1,0:T(4,128)S(1)} %get-tuple-element.7, f32[3,4096]{1,0:T(4,128)S(1)} %get-tuple-element.6, f32[3,4096]{1,0:T(4,128)S(1)} %get-tuple-element.5), kind=kLoop, calls=%fused_computation.1 | loop fusion | flops 7864320 | bytes 25313280 | tf_op jit(solution)/shard_map/add | solution.py:28
  33.5 2.6 %copy-done = f32[128,3,4096]{0,2,1:T(8,128)} copy-done((f32[128,3,4096]{0,2,1:T(8,128)}, f32[128,3,4096]{0,2,1:T(8,128)S(1)}, u32[]{:S(2)}) %copy-start) | copy-done | bytes 6291480
  36.1 0.2 fusion.2
  36.3 0.5 copy.21
  36.8 16.9 %all_to_all.29 = bf16[128,4,1024]{2,0,1:T(8,128)(2,1)S(1)} all-to-all(bf16[128,4,1024]{2,0,1:T(8,128)(2,1)S(1)} %copy.21), channel_id=1, replica_groups=mesh['dp'=8,'ctx'=4] {'ctx'}, dimensions={1} | all-to-all | bytes 2097152 | tf_op jit(solution)/shard_map/all_to_all | solution.py:176
  53.7 0.8 copy.22
  54.5 0.3 reshape.46
  54.8 4.5 %fusion.8 = f32[1024,1024]{1,0:T(8,128)} fusion(bf16[1024,512]{1,0:T(8,128)(2,1)} %constant.39, bf16[512,1024]{1,0:T(8,128)(2,1)S(1)} %reshape.46), kind=kOutput, calls=%fused_computation.31 | convolution fusion | flops 1073741824 | bytes 6291456 | tf_op jit(solution)/shard_map/dot_general | solution.py:141
  59.3 2.9 %fusion.9 = f32[1024,1024]{1,0:T(8,128)S(1)} fusion(bf16[1024,512]{1,0:T(8,128)(2,1)} %constant.34.clone, bf16[512,1024]{1,0:T(8,128)(2,1)} %all-gather.2.cloned.1.call-done), kind=kOutput, calls=%fused_computation.32 | convolution fusion | flops 1073741824 | bytes 6291456 | tf_op jit(solution)/shard_map/dot_general | solution.py:142
  62.3 0.8 fusion.6
  63.1 0.2 copy-done.2
  63.4 0.9 fusion.4
  64.2 16.9 %all_to_all.30 = bf16[4,128,1024]{2,1,0:T(8,128)(2,1)S(1)} all-to-all(bf16[4,128,1024]{2,1,0:T(8,128)(2,1)S(1)} %bitcast.38), channel_id=1, replica_groups=mesh['dp'=8,'ctx'=4] {'ctx'}, dimensions={0} | all-to-all | bytes 2097152 | tf_op jit(solution)/shard_map/all_to_all | solution.py:178
  81.1 1.6 %convert_bitcast_fusion = f32[128,4,1024]{2,0,1:T(8,128)} fusion(bf16[4,128,1024]{2,1,0:T(8,128)(2,1)S(1)} %all_to_all.30), kind=kLoop, calls=%fused_computation.14 | loop fusion | flops 524288 | bytes 3145728 | tf_op jit(solution)/shard_map/convert_element_type | solution.py:163
  82.7 1.9 %copy.23 = f32[128,4,1024]{0,2,1:T(8,128)S(1)} copy(f32[128,4,1024]{2,0,1:T(8,128)} %convert_bitcast_fusion) | data formatting | bytes 4194304 | tf_op jit(solution)/shard_map/convert_element_type | solution.py:163
  84.6 2.0 %fusion.5 = bf16[1,128,4096]{1,2,0:T(8,128)(2,1)S(1)} fusion(f32[128,4,1024]{0,2,1:T(8,128)S(1)} %copy.23, f32[128,3,4096]{0,2,1:T(8,128)} %copy-done), kind=kLoop, calls=%fused_computation.13 | loop fusion | flops 1572864 | bytes 4194304 | tf_op jit(solution)/shard_map/convert_element_type | solution.py:163
  86.7 1.3 %copy.24 = bf16[1,128,4096]{2,1,0:T(8,128)(2,1)} copy(bf16[1,128,4096]{1,2,0:T(8,128)(2,1)S(1)} %fusion.5) | data formatting | bytes 2097152 | tf_op jit(solution)/shard_map/convert_element_type | solution.py:163
  (27 shorter events, 0.3 us)
Async XLA Ops:
  6.5 52.8 %all-gather.2.cloned.1.call-start = ((), (), s32[]{:S(2)}) async-start(), calls=%async_computation.2 | async-start | bytes 1179648 | tf_op jit(solution)/shard_map/all_gather | solution.py:170
  6.5 6.0 %collective-permute-start = (f32[3,3,1024]{2,1,0:T(4,128)}, f32[3,3,1024]{2,1,0:T(4,128)S(1)}, u32[]{:S(2)}, u32[]{:S(2)}) collective-permute-start(f32[3,3,1024]{2,1,0:T(4,128)} %param.7), channel_id=1, source_target_pairs={{0,1},{1,2},{2,3},{3,0},{4,5},{5,6},{6,7},{7,4},{8,9},{9,10},{10,1... | collective-permute-start | bytes 110600 | tf_op jit(solution)/shard_map/ppermute | solution.py:16
  8.0 8.1 %collective-permute-start.3 = (bf16[2,3,4096]{2,0,1:T(2,128)(2,1)S(1)}, bf16[2,3,4096]{2,0,1:T(2,128)(2,1)S(1)}, u32[]{:S(2)}, u32[]{:S(2)}) collective-permute-start(bf16[2,3,4096]{2,0,1:T(2,128)(2,1)S(1)} %slice_bitcast_fusion), channel_id=1, source_target_pairs={{0,1},{1,2},{2,3},{4,5},{5,6},{6,7},{8,9},{9,10},{10,11},{12,13},{... | collective-permute-start | bytes 147464 | tf_op jit(solution)/shard_map/ppermute | solution.py:172
  12.5 6.4 %collective-permute-start.1 = (f32[3,3,1024]{2,1,0:T(4,128)S(1)}, f32[3,3,1024]{2,1,0:T(4,128)S(1)}, u32[]{:S(2)}, u32[]{:S(2)}) collective-permute-start(f32[3,3,1024]{2,1,0:T(4,128)S(1)} %collective-permute-done), channel_id=1, source_target_pairs={{0,1},{1,2},{2,3},{3,0},{4,5},{5,6},{6,7},{7,4},{8,9},{9,10},{10,1... | collective-permute-start | bytes 110600 | tf_op jit(solution)/shard_map/ppermute | solution.py:16
  18.9 4.9 %collective-permute-start.2 = (f32[3,3,1024]{2,1,0:T(4,128)S(1)}, f32[3,3,1024]{2,1,0:T(4,128)S(1)}, u32[]{:S(2)}, u32[]{:S(2)}) collective-permute-start(f32[3,3,1024]{2,1,0:T(4,128)S(1)} %collective-permute-done.1), channel_id=1, source_target_pairs={{0,1},{1,2},{2,3},{3,0},{4,5},{5,6},{6,7},{7,4},{8,9},{9,10},{10,1... | collective-permute-start | bytes 110600 | tf_op jit(solution)/shard_map/ppermute | solution.py:16
  19.7 4.2 %copy-start.4 = (f32[3,3,1024]{2,1,0:T(4,128)S(1)}, f32[3,3,1024]{2,1,0:T(4,128)}, u32[]{:S(2)}) copy-start(f32[3,3,1024]{2,1,0:T(4,128)} %param.7) | copy-start | bytes 110596
  33.4 2.6 %copy-start = (f32[128,3,4096]{0,2,1:T(8,128)}, f32[128,3,4096]{0,2,1:T(8,128)S(1)}, u32[]{:S(2)}) copy-start(f32[128,3,4096]{0,2,1:T(8,128)S(1)} %fusion) | copy-start | bytes 18874372
  59.3 3.0 %copy-start.3 = (bf16[512,512]{1,0:T(8,128)(2,1)S(1)}, bf16[512,512]{1,0:T(8,128)(2,1)}, u32[]{:S(2)}) copy-start(bf16[512,512]{1,0:T(8,128)(2,1)} %constant.40) | copy-start | bytes 1572868
  59.3 3.0 %copy-start.1 = (f32[1024,1024]{1,0:T(8,128)S(1)}, f32[1024,1024]{1,0:T(8,128)}, u32[]{:S(2)}) copy-start(f32[1024,1024]{1,0:T(8,128)} %fusion.8) | copy-start | bytes 12582916
  62.3 1.0 %copy-start.2 = (bf16[512,512]{1,0:T(8,128)(2,1)S(1)}, bf16[512,512]{1,0:T(8,128)(2,1)}, u32[]{:S(2)}) copy-start(bf16[512,512]{1,0:T(8,128)(2,1)} %constant.41) | copy-start | bytes 1572868
  62.3 1.0 %copy-start.5 = (f32[1024]{0:T(1024)S(1)}, f32[1024]{0:T(1024)}, u32[]{:S(2)}) copy-start(f32[1024]{0:T(1024)} %param.9) | copy-start | bytes 12292
Sparse Core Ops, SparseCore 0:
  12.7 41.7 all-gather.1
